TPU v7x, 32 devices: a whole 2x2x4 slice. The times are simulated.
32 devices in a mesh: dp: 8 (over z, y), seq: 4 (over x, core).
Axes of the slice: x: 2, y: 2, z: 4, core: 2. Of those that a mesh axis runs over, the one named last changes fastest.
Arguments:
- hidden: bfloat16 [16, 2048, 768], P('dp', 'seq'), may hold values from -6 to 6
- lengths: int32 [16], P('dp'), may hold values from 512 to 2048
- norm_gain: float32 [768], P(('dp', 'seq')), may hold values from 0.5 to 1.5
- in_weight: float32 [768, 3352], P(('dp', 'seq')), may hold values from -0.21875 to 0.21875
- conv_weight: float32 [4, 1792], P(None, ('dp', 'seq')), may hold values from -3 to 3
- conv_bias: float32 [1792], P(('dp', 'seq')), may hold values from -2.5 to 2.5
- step_bias: float32 [24], replicated, may hold values from -10 to -5
- decay_log: float32 [24], replicated, may hold values from 0 to 1
- skip_gain: float32 [24], replicated, may hold values from 0.5 to 1.5
- gate_gain: float32 [1536], P(('dp', 'seq')), may hold values from 0.5 to 1.5
- out_weight: float32 [1536, 768], P(('dp', 'seq')), may hold values from -0.15625 to 0.15625
- cotangent: bfloat16 [16, 2048, 768], P('dp', 'seq'), may hold values from -6 to 6
Outputs:
- output: bfloat16 [16, 2048, 768], P('dp', 'seq')
- grad_hidden: bfloat16 [16, 2048, 768], P('dp', 'seq')
- grad_norm_gain: float32 [768], P(('dp', 'seq'))
- grad_in_weight: float32 [768, 3352], P(('dp', 'seq'))
- grad_conv_weight: float32 [4, 1792], P(None, ('dp', 'seq'))
- grad_conv_bias: float32 [1792], P(('dp', 'seq'))
- grad_step_bias: float32 [24], replicated
- grad_decay_log: float32 [24], replicated
- grad_skip_gain: float32 [24], replicated
- grad_gate_gain: float32 [1536], P(('dp', 'seq'))
- grad_out_weight: float32 [1536, 768], P(('dp', 'seq'))
All inputs are finite; a program needn't handle non-finite values.
Results may differ from a plain program's by a relative error of at most 0.00435.
The roundings to bfloat16 on the way count: a program that leaves them out, or rounds other values in their place, can miss the bound.
Values may be sent and summed in bfloat16 or wider, within the bound.
No kernel may reach another device: no remote copies, remote signals or barrier semaphores. Data moves between devices by JAX's collectives and lax.ppermute only.
A program may use at most 192 MiB of HBM per device.

v0:
```python
import jax
import jax.numpy as jnp
from jax import lax
from jax.sharding import PartitionSpec as P

H = 24
P_SIZE = 64
N = 128
KW = 4
Q = 256
DI = 1536
CD = 1792
epsilon = 1e-05


def from_behind(block, axis, distance):
    devices = range(lax.axis_size(axis))
    route = [(i - distance, i) for i in devices if i - distance in devices]
    return lax.ppermute(block, axis, route)


def rms_scale(values):
    return lax.rsqrt(jnp.mean(values * values, axis=-1, keepdims=True) + epsilon)


def decay_matrix(cum_group):
    width_q = cum_group.shape[-1]
    lower = jnp.arange(width_q)[:, None] >= jnp.arange(width_q)[None, :]
    gap = jnp.where(lower[None], cum_group[:, :, None] - cum_group[:, None, :], 0.0)
    return jnp.where(lower[None], jnp.exp(gap), 0.0)


def intra_forward(group_item):
    x_group, b_group, c_group, step_group, cum_group = group_item
    scores = jnp.einsum("qn,rn->qr", c_group, b_group, preferred_element_type=jnp.float32)
    mixing = (scores[None] * decay_matrix(cum_group) * step_group[:, None, :]).astype(jnp.bfloat16)
    return jnp.einsum("hqr,rhp->qhp", mixing, x_group, preferred_element_type=jnp.float32)


def intra_backward(group_item):
    x_group, b_group, c_group, step_group, cum_group, grad_group = group_item
    scores = jnp.einsum("qn,rn->qr", c_group, b_group, preferred_element_type=jnp.float32)
    spread = decay_matrix(cum_group)
    rate_weight = spread * step_group[:, None, :]
    mixing = (scores[None] * rate_weight).astype(jnp.bfloat16)
    grad_mixing = jnp.einsum(
        "qhp,rhp->hqr", grad_group, x_group, preferred_element_type=jnp.float32
    )
    grad_x = jnp.einsum("hqr,qhp->rhp", mixing, grad_group, preferred_element_type=jnp.float32)
    grad_scores = jnp.sum(grad_mixing * rate_weight, axis=0).astype(jnp.bfloat16)
    grad_c = jnp.einsum("qr,rn->qn", grad_scores, b_group, preferred_element_type=jnp.float32)
    grad_b = jnp.einsum("qr,qn->rn", grad_scores, c_group, preferred_element_type=jnp.float32)
    through = grad_mixing * scores[None] * spread
    cum_flow = through * step_group[:, None, :]
    grad_cum = jnp.sum(cum_flow, axis=2) - jnp.sum(cum_flow, axis=1)
    return (grad_x, grad_b, grad_c, jnp.sum(through, axis=1), grad_cum)


def per_device(
    hidden,
    lengths,
    norm_gain,
    in_weight,
    conv_weight,
    conv_bias,
    step_bias,
    decay_log,
    skip_gain,
    gate_gain,
    out_weight,
    cotangent,
):
    seq_count, piece_len, model_width = hidden.shape
    group_count = piece_len // Q
    block_count = seq_count * group_count
    token_rows = seq_count * piece_len
    halo_width = KW - 1
    shards = (
        norm_gain.astype(jnp.bfloat16),
        in_weight.astype(jnp.bfloat16),
        conv_weight.astype(jnp.bfloat16),
        conv_bias.astype(jnp.bfloat16),
        gate_gain.astype(jnp.bfloat16),
        out_weight.astype(jnp.bfloat16),
    )
    gathered = (
        lax.all_gather(shards[0], ("dp", "seq"), axis=0, tiled=True),
        lax.all_gather(shards[1], ("dp", "seq"), axis=0, tiled=True),
        lax.all_gather(shards[2], ("dp", "seq"), axis=1, tiled=True),
        lax.all_gather(shards[3], ("dp", "seq"), axis=0, tiled=True),
        lax.all_gather(shards[4], ("dp", "seq"), axis=0, tiled=True),
        lax.all_gather(shards[5], ("dp", "seq"), axis=0, tiled=True),
    )
    gain_in, in_full, kernel_full, bias_full, gain_gate, out_full = gathered
    positions = lax.axis_index("seq") * piece_len + jnp.arange(piece_len, dtype=jnp.int32)
    valid_mask = (positions[None, :] < lengths[:, None]).astype(jnp.float32)
    x_float = hidden.astype(jnp.float32)
    scale_in = rms_scale(x_float)
    normed = (
        (x_float * scale_in * gain_in.astype(jnp.float32))
        .astype(jnp.bfloat16)
        .reshape(token_rows, model_width)
    )
    projected = jnp.dot(normed, in_full, preferred_element_type=jnp.float32).reshape(
        seq_count, piece_len, -1
    )
    gate_z = projected[..., :DI]
    conv_in = projected[..., DI : DI + CD].astype(jnp.bfloat16)
    dt_raw = projected[..., DI + CD :]
    rim_rows = from_behind(conv_in[:, piece_len - halo_width :, :], "seq", 1)
    extended = jnp.concatenate([rim_rows, conv_in], axis=1)
    kernel = kernel_full.astype(jnp.float32)
    pre_act = bias_full.astype(jnp.float32) + sum(
        (
            kernel[offset] * extended[:, offset : offset + piece_len].astype(jnp.float32)
            for offset in range(KW)
        )
    )
    conv_out = jax.nn.silu(pre_act)
    x_heads = conv_out[..., :DI].astype(jnp.bfloat16).reshape(block_count, Q, H, P_SIZE)
    b_rows = conv_out[..., DI : DI + N].astype(jnp.bfloat16).reshape(block_count, Q, N)
    c_rows = conv_out[..., DI + N :].astype(jnp.bfloat16).reshape(block_count, Q, N)
    step_size = jax.nn.softplus(dt_raw + step_bias)
    decay_rate = jnp.exp(decay_log)
    step_blocks = step_size.reshape(block_count, Q, H).transpose(0, 2, 1)
    cum_decay = jnp.cumsum(-step_blocks * decay_rate[None, :, None], axis=2)
    intra_out = lax.map(intra_forward, (x_heads, b_rows, c_rows, step_blocks, cum_decay))
    tail_weight = jnp.exp(cum_decay[:, :, -1:] - cum_decay) * step_blocks
    b_scaled = (b_rows[:, None].astype(jnp.float32) * tail_weight[..., None]).astype(jnp.bfloat16)
    local_state = jnp.einsum(
        "bhqn,bqhp->bhnp", b_scaled, x_heads, preferred_element_type=jnp.float32
    )
    block_decay = jnp.exp(cum_decay[:, :, -1])
    group_decay = block_decay.reshape(seq_count, group_count, H)
    local_parts = local_state.reshape(seq_count, group_count, H, N, P_SIZE)
    running = jnp.zeros((seq_count, H, N, P_SIZE), jnp.float32)
    carried = jnp.ones((seq_count, H), jnp.float32)
    start_list = []
    prefix_list = []
    for block_index in range(group_count):
        start_list.append(running)
        prefix_list.append(carried)
        running = group_decay[:, block_index, :, None, None] * running + local_parts[:, block_index]
        carried = carried * group_decay[:, block_index]
    incoming = jnp.zeros_like(running)
    for rounds in range(lax.axis_size("seq") - 1):
        incoming = from_behind(carried[:, :, None, None] * incoming + running, "seq", 1)
    group_starts = jnp.stack(
        [
            start_list[block_index] + prefix_list[block_index][:, :, None, None] * incoming
            for block_index in range(group_count)
        ],
        axis=1,
    ).reshape(block_count, H, N, P_SIZE)
    growth = jnp.exp(cum_decay)
    c_scaled = c_rows[:, None].astype(jnp.float32) * growth[..., None]
    c_low = c_scaled.astype(jnp.bfloat16)
    starts_low = group_starts.astype(jnp.bfloat16)
    inter_out = jnp.einsum("bhqn,bhnp->bqhp", c_low, starts_low, preferred_element_type=jnp.float32)
    ssm_out = (
        intra_out + inter_out + skip_gain[None, None, :, None] * x_heads.astype(jnp.float32)
    ).reshape(seq_count, piece_len, DI)
    gate_sig = jax.nn.sigmoid(gate_z)
    gated_out = ssm_out * gate_z * gate_sig
    scale_gate = rms_scale(gated_out)
    gated_norm = (
        (gated_out * scale_gate * gain_gate.astype(jnp.float32))
        .astype(jnp.bfloat16)
        .reshape(token_rows, DI)
    )
    branch = jnp.dot(gated_norm, out_full, preferred_element_type=jnp.float32).reshape(
        seq_count, piece_len, model_width
    )
    output = (x_float + valid_mask[..., None] * branch).astype(jnp.bfloat16)
    back_shards = (shards[0], shards[1], shards[2], shards[4], shards[5])
    back_weights = (
        lax.all_gather(back_shards[0], ("dp", "seq"), axis=0, tiled=True),
        lax.all_gather(back_shards[1], ("dp", "seq"), axis=0, tiled=True),
        lax.all_gather(back_shards[2], ("dp", "seq"), axis=1, tiled=True),
        lax.all_gather(back_shards[3], ("dp", "seq"), axis=0, tiled=True),
        lax.all_gather(back_shards[4], ("dp", "seq"), axis=0, tiled=True),
    )
    gain_in_back, in_back, kernel_back, gain_gate_back, out_back = back_weights
    d_branch = (
        (cotangent.astype(jnp.float32) * valid_mask[..., None])
        .astype(jnp.bfloat16)
        .reshape(token_rows, model_width)
    )
    grad_out = jnp.einsum("tk,td->kd", gated_norm, d_branch, preferred_element_type=jnp.float32)
    grad_norm_out = jnp.einsum(
        "td,kd->tk", d_branch, out_back, preferred_element_type=jnp.float32
    ).reshape(seq_count, piece_len, DI)
    grad_gate_gain = jnp.sum(grad_norm_out * gated_out * scale_gate, axis=(0, 1))
    scaled_back = grad_norm_out * gain_gate_back.astype(jnp.float32)
    grad_gated = scale_gate * scaled_back - gated_out * (
        scale_gate * scale_gate * scale_gate
    ) * jnp.mean(scaled_back * gated_out, axis=-1, keepdims=True)
    grad_ssm = (grad_gated * gate_z * gate_sig).astype(jnp.bfloat16)
    grad_gate_z = grad_gated * ssm_out * gate_sig * (1.0 + gate_z * (1.0 - gate_sig))
    grad_blocks = grad_ssm.reshape(block_count, Q, H, P_SIZE)
    grad_skip = jnp.einsum("bqhp,bqhp->h", grad_blocks, x_heads, preferred_element_type=jnp.float32)
    intra_x, intra_b, intra_c, intra_step, intra_cum = lax.map(
        intra_backward, (x_heads, b_rows, c_rows, step_blocks, cum_decay, grad_blocks)
    )
    grad_in_y = jnp.einsum(
        "bhqn,bqhp->bhnp", c_low, grad_blocks, preferred_element_type=jnp.float32
    ).reshape(seq_count, group_count, H, N, P_SIZE)
    back_running = jnp.zeros((seq_count, H, N, P_SIZE), jnp.float32)
    for block_index in reversed(range(group_count)):
        back_running = (
            group_decay[:, block_index, :, None, None] * back_running + grad_in_y[:, block_index]
        )
    arriving = jnp.zeros_like(back_running)
    for rounds in range(lax.axis_size("seq") - 1):
        arriving = from_behind(carried[:, :, None, None] * arriving + back_running, "seq", -1)
    end_list = [None] * group_count
    following = arriving
    for block_index in reversed(range(group_count)):
        end_list[block_index] = following
        following = (
            group_decay[:, block_index, :, None, None] * following + grad_in_y[:, block_index]
        )
    grad_end = jnp.stack(end_list, axis=1).reshape(block_count, H, N, P_SIZE)
    grad_last = jnp.sum(grad_end * group_starts, axis=(2, 3)) * block_decay
    grad_local = grad_end.astype(jnp.bfloat16)
    grad_b_scaled = jnp.einsum(
        "bqhp,bhnp->bhqn", x_heads, grad_local, preferred_element_type=jnp.float32
    )
    grad_x_heads = (
        skip_gain[None, None, :, None] * grad_blocks.astype(jnp.float32)
        + intra_x
        + jnp.einsum("bhqn,bhnp->bqhp", b_scaled, grad_local, preferred_element_type=jnp.float32)
    )
    grad_b = intra_b + jnp.einsum("bhqn,bhq->bqn", grad_b_scaled, tail_weight)
    grad_tail = jnp.einsum("bhqn,bqn->bhq", grad_b_scaled, b_rows.astype(jnp.float32))
    tail_flow = grad_tail * tail_weight
    grad_step = intra_step + grad_tail * jnp.exp(cum_decay[:, :, -1:] - cum_decay)
    grad_c_scaled = jnp.einsum(
        "bqhp,bhnp->bhqn", grad_blocks, starts_low, preferred_element_type=jnp.float32
    )
    grad_c = intra_c + jnp.einsum("bhqn,bhq->bqn", grad_c_scaled, growth)
    grad_cum = intra_cum - tail_flow + jnp.einsum("bhqn,bhqn->bhq", grad_c_scaled, c_scaled)
    grad_cum = grad_cum.at[:, :, -1].add(grad_last + jnp.sum(tail_flow, axis=2))
    grad_log = lax.cumsum(grad_cum, axis=2, reverse=True)
    grad_step = grad_step - grad_log * decay_rate[None, :, None]
    grad_decay = -jnp.sum(grad_log * step_blocks, axis=(0, 2)) * decay_rate
    grad_step_tokens = grad_step.transpose(0, 2, 1).reshape(seq_count, piece_len, H)
    grad_dt_raw = grad_step_tokens * jax.nn.sigmoid(dt_raw + step_bias)
    grad_step_bias = jnp.sum(grad_dt_raw, axis=(0, 1))
    grad_conv_out = jnp.concatenate(
        [
            grad_x_heads.reshape(seq_count, piece_len, DI),
            grad_b.reshape(seq_count, piece_len, N),
            grad_c.reshape(seq_count, piece_len, N),
        ],
        axis=-1,
    )
    pre_sig = jax.nn.sigmoid(pre_act)
    grad_pre = grad_conv_out * pre_sig * (1.0 + pre_act * (1.0 - pre_sig))
    grad_conv_bias = jnp.sum(grad_pre, axis=(0, 1))
    grad_kernel = jnp.stack(
        [
            jnp.sum(
                grad_pre * extended[:, offset : offset + piece_len].astype(jnp.float32), axis=(0, 1)
            )
            for offset in range(KW)
        ],
        axis=0,
    )
    kernel_float = kernel_back.astype(jnp.float32)
    grad_ext = sum(
        (
            jnp.pad(
                kernel_float[offset] * grad_pre, ((0, 0), (offset, halo_width - offset), (0, 0))
            )
            for offset in range(KW)
        )
    )
    returned = from_behind(grad_ext[:, :halo_width].astype(jnp.bfloat16), "seq", -1).astype(
        jnp.float32
    )
    grad_conv_in = grad_ext[:, halo_width:] + jnp.pad(
        returned, ((0, 0), (piece_len - halo_width, 0), (0, 0))
    )
    grad_proj = (
        jnp.concatenate([grad_gate_z, grad_conv_in, grad_dt_raw], axis=-1)
        .astype(jnp.bfloat16)
        .reshape(token_rows, -1)
    )
    grad_in = jnp.einsum("td,te->de", normed, grad_proj, preferred_element_type=jnp.float32)
    grad_normed = jnp.einsum(
        "te,de->td", grad_proj, in_back, preferred_element_type=jnp.float32
    ).reshape(seq_count, piece_len, model_width)
    grad_norm_gain = jnp.sum(grad_normed * x_float * scale_in, axis=(0, 1))
    scaled_in = grad_normed * gain_in_back.astype(jnp.float32)
    grad_x_in = scale_in * scaled_in - x_float * (scale_in * scale_in * scale_in) * jnp.mean(
        scaled_in * x_float, axis=-1, keepdims=True
    )
    grad_hidden = (cotangent.astype(jnp.float32) + grad_x_in).astype(jnp.bfloat16)
    owned_grads = (
        lax.psum_scatter(grad_norm_gain, ("dp", "seq"), scatter_dimension=0, tiled=True),
        lax.psum_scatter(grad_in, ("dp", "seq"), scatter_dimension=0, tiled=True),
        lax.psum_scatter(grad_kernel, ("dp", "seq"), scatter_dimension=1, tiled=True),
        lax.psum_scatter(grad_conv_bias, ("dp", "seq"), scatter_dimension=0, tiled=True),
        lax.psum_scatter(grad_gate_gain, ("dp", "seq"), scatter_dimension=0, tiled=True),
        lax.psum_scatter(grad_out, ("dp", "seq"), scatter_dimension=0, tiled=True),
    )
    head_totals = lax.psum((grad_step_bias, grad_decay, grad_skip), ("dp", "seq"))
    return (
        output,
        grad_hidden,
        owned_grads[0],
        owned_grads[1],
        owned_grads[2],
        owned_grads[3],
        head_totals[0],
        head_totals[1],
        head_totals[2],
        owned_grads[4],
        owned_grads[5],
    )


def solution(mesh):
    return jax.shard_map(
        per_device,
        mesh=mesh,
        in_specs=(
            P("dp", "seq", None),
            P("dp"),
            P(("dp", "seq")),
            P(("dp", "seq"), None),
            P(None, ("dp", "seq")),
            P(("dp", "seq")),
            P(),
            P(),
            P(),
            P(("dp", "seq")),
            P(("dp", "seq"), None),
            P("dp", "seq", None),
        ),
        out_specs=(
            P("dp", "seq", None),
            P("dp", "seq", None),
            P(("dp", "seq")),
            P(("dp", "seq"), None),
            P(None, ("dp", "seq")),
            P(("dp", "seq")),
            P(),
            P(),
            P(),
            P(("dp", "seq")),
            P(("dp", "seq"), None),
        ),
        check_vma=False,
    )
```

profile of v0, /device:TPU:0, one launch (start us, length us, event | category | flops | bytes accessed | tf_op | source)
XLA Modules:
  0.0 762.1 jit_solution(16280473056816043643)
XLA Ops:
  12.2 42.3 %all-reduce.14 = (bf16[768]{0:T(1024)(128)(2,1)S(1)}, bf16[1792]{0:T(1024)(128)(2,1)S(1)}, bf16[1536]{0:T(1024)(128)(2,1)S(1)}) all-reduce(bf16[768]{0:T(1024)(128)(2,1)S(1)} %dynamic-update-slice.4, bf16[1792]{0:T(1024)(128)(2,1)S(1)} %dynamic-update-slice.3, ...), channel_id=1, replica_groups=mesh['dp'=8,'seq'=4] {'dp','seq'}, use_global_device_ids=true, to_apply=%add.6 | all-reduce | flops 4096 | bytes 16384
  55.2 40.5 %all-gather = bf16[32,56,4]{1,2,0:T(4,128)(2,1)S(1)} all-gather(bf16[1,56,4]{1,2,0:T(4,128)(2,1)S(1)} %convert_bitcast_fusion), channel_id=1, replica_groups=mesh['dp'=8,'seq'=4] {'dp','seq'}, dimensions={0}, use_global_device_ids=true | all-gather | bytes 14784 | tf_op jit(solution)/shard_map/all_gather | solution.py:89
  98.4 12.8 %fusion.145 = (bf16[2,512,3352]{1,2,0:T(8,128)(2,1)}, f32[2,512,3352]{1,2,0:T(8,128)}) fusion(bf16[768,3352]{1,0:T(8,128)(2,1)} %all-gather.4.cloned.1.call-done, bf16[2,512,768]{2,1,0:T(8,128)(2,1)} %param.18, f32[768]{0:T(1024)S(1)} %convert_element_type.157, f32[2,512]{1,0:T(2,128)S(1)} %get-tuple-element.308), kind=kOutput, calls=%fused_computation.256 | convolution fusion | flops 5278818304 | bytes 27323392 | tf_op jit(solution)/shard_map/dot_general | solution.py:104
  127.4 12.4 %multiply_convert_fusion.14 = (bf16[2,512,1792]{1,2,0:T(8,128)(2,1)S(1)}, f32[2,512,1792]{1,2,0:T(8,128)}) fusion(bf16[2,512,1792]{1,2,0:T(8,128)(2,1)} %slice.154, f32[1792]{0:T(1024)S(1)} %get-tuple-element.225, bf16[2,3,1792]{1,2,0:T(8,128)(2,1)S(1)} %copy.159, f32[1792]{0:T(1024)S(1)} %get-tuple-element.226, f32[1792]{0:T(1024)S(1)} %get-tuple-element.227, ...), kind=kLoop, calls=%fused_computation.107 | loop fusion | flops 47710208 | bytes 14737408 | tf_op jit(solution)/shard_map/convert.8
  140.9 14.5 %copy.160 = bf16[2,512,1536]{1,0,2:T(2,128)(2,1)} copy(bf16[2,512,1536]{1,2,0:T(8,128)(2,1)S(1)} %slice.162) | data formatting | bytes 6291456 | tf_op jit(solution)/shard_map/slice | solution.py:120
  176.1 17.4 %collective-permute-start.2 = (f32[2,24,128,64]{2,3,1,0:T(8,128)}, f32[2,24,128,64]{2,3,1,0:T(8,128)}, u32[]{:S(2)}, u32[]{:S(2)}) collective-permute-start(f32[2,24,128,64]{2,3,1,0:T(8,128)} %multiply_add_fusion.3), channel_id=1, source_target_pairs={{0,1},{1,2},{2,3},{4,5},{5,6},{6,7},{8,9},{9,10},{10,11},{12,13},{... | collective-permute-start | bytes 4718600 | tf_op jit(solution)/shard_map/ppermute | solution.py:19
  203.8 15.6 %collective-permute-start.3 = (f32[2,24,128,64]{2,3,1,0:T(8,128)}, f32[2,24,128,64]{2,3,1,0:T(8,128)}, u32[]{:S(2)}, u32[]{:S(2)}) collective-permute-start(f32[2,24,128,64]{2,3,1,0:T(8,128)} %multiply_add_fusion.2), channel_id=1, source_target_pairs={{0,1},{1,2},{2,3},{4,5},{5,6},{6,7},{8,9},{9,10},{10,11},{12,13},{... | collective-permute-start | bytes 4718600 | tf_op jit(solution)/shard_map/ppermute | solution.py:19
  222.9 25.0 %while.29 = (s32[]{:T(128)}, f32[4,256,24,64]{1,3,2,0:T(8,128)}, bf16[4,256,24,64]{1,3,2,0:T(8,128)(2,1)}, bf16[4,256,128]{2,1,0:T(8,128)(2,1)}, bf16[4,256,128]...) while((s32[]{:T(128)}, f32[4,256,24,64]{1,3,2,0:T(8,128)}, ...), condition=%wide.region_4.5_spmd, body=%wide.region_3.4_spmd.sunk | while | flops 227606528 | bytes 3319905 | solution.py:127
  265.9 9.3 %reshape.314 = f32[2,512,1536]{1,0,2:T(2,128)} reshape(f32[4,256,24,64]{1,0,3,2:T(4,128)} %copy.179) | data formatting | bytes 12582912 | tf_op jit(solution)/shard_map/reshape | solution.py:162
  282.8 10.6 %multiply_reduce_fusion.3 = (f32[1536]{0:T(1024)}, f32[2,512]{1,0:T(2,128)S(1)}, f32[2,512,1536]{1,2,0:T(8,128)}) fusion(f32[2,512,1536]{1,2,0:T(8,128)} %get-tuple-element.282, f32[2,512]{1,0:T(2,128)S(1)} %get-tuple-element.310, f32[1536]{0:T(1024)S(1)} %convert_element_type.172, bf16[1536,768]{1,0:T(8,128)(2,1)} %all-gather.6.cloned.1.call-done, ...), kind=kOutput, calls=%fused_computation.121 | convolution fusion | flops 2427713024 | bytes 16539648 | tf_op jit(solution)/shard_map/td,kd->tk/dot_general | solution.py:190
  293.5 8.8 %multiply_convert_fusion.16 = (bf16[2,512,1536]{1,2,0:T(8,128)(2,1)}, bf16[2,512,1536]{1,2,0:T(8,128)(2,1)S(1)}) fusion(f32[2,512,1536]{1,0,2:T(2,128)S(1)} %copy-done, f32[2,512,3352]{1,2,0:T(8,128)} %get-tuple-element.316, f32[2,512]{1,0:T(2,128)S(1)} %broadcast_multiply_fusion.4, f32[2,512,1536]{1,2,0:T(8,128)S(1)} %copy-done.2, ...), kind=kLoop, calls=%fused_computation.123 | loop fusion | flops 28311552 | bytes 31475712 | tf_op jit(solution)/shard_map/convert.2
  302.2 14.4 %copy.184 = bf16[2,512,1536]{1,0,2:T(2,128)(2,1)} copy(bf16[2,512,1536]{1,2,0:T(8,128)(2,1)S(1)} %get-tuple-element.294) | data formatting | bytes 6291456 | tf_op jit(solution)/shard_map/convert_element_type | solution.py:198
  371.4 61.5 %while.30 = (s32[]{:T(128)}, f32[4,256,24,64]{1,3,2,0:T(8,128)}, f32[4,256,128]{2,1,0:T(8,128)}, f32[4,256,128]{2,1,0:T(8,128)}, f32[4,24,256]{2,1,0:T(8,128)}, ...) while((s32[]{:T(128)}, f32[4,256,24,64]{1,3,2,0:T(8,128)}, ...), condition=%wide.region_12.13_spmd, body=%wide.region_7.12_spmd.sunk | while | flops 481284096 | bytes 6280337 | solution.py:202
  436.7 10.9 %fusion.52 = (f32[4,24,256]{2,1,0:T(8,128)}, bf16[4,24,256,128]{3,2,1,0:T(8,128)(2,1)S(1)}) fusion(f32[4,24,256]{2,1,0:T(8,128)S(1)} %copy-done.36, f32[4,256,128]{2,1,0:T(8,128)} %copy-done.23, bf16[4,24,128,64]{2,3,1,0:T(8,128)(2,1)} %bitcast.288, bf16[4,256,24,64]{1,0,3,2:T(4,128)(2,1)} %reshape.315), kind=kOutput, calls=%fused_computation.73 | convolution fusion | flops 415211520 | bytes 11730944 | tf_op jit(solution)/shard_map/bqhp,bhnp->bhqn/dot_general | solution.py:238
  491.0 9.4 %reshape.317 = f32[2,512,1536]{1,0,2:T(2,128)} reshape(f32[4,256,24,64]{1,0,3,2:T(4,128)} %copy.193) | data formatting | bytes 12582912 | tf_op jit(solution)/shard_map/reshape | solution.py:252
  511.0 10.0 %reduce-window.16 = f32[4,24,2,128]{3,1,2,0:T(8,128)S(1)} reduce-window(f32[4,24,2,128]{3,1,2,0:T(8,128)S(1)} %copy.206, f32[]{:T(128)} %constant.98.clone.1), window={size=1x1x1x128 pad=0_0x0_0x0_0x0_127}, to_apply=%region_15.16 | reduce-window | flops 3121152 | bytes 196612 | tf_op jit(solution)/shard_map/reduce-window.2
  527.3 19.6 %fusion.137 = (f32[1792]{0:T(1024)}, f32[1792]{0:T(1024)}, f32[1792]{0:T(1024)}, f32[1792]{0:T(1024)}, f32[1792]{0:T(1024)}, /*index=5*/f32[2,512,1792]{1,2,0:T(8,128)S(1)}) fusion(bf16[2,512,3352]{1,2,0:T(8,128)(2,1)} %get-tuple-element.315, bf16[2,512,1792]{1,2,0:T(8,128)(2,1)} %slice.154, bf16[2,3,1792]{1,2,0:T(8,128)(2,1)} %copy-done.8, ...), kind=kLoop, calls=%fused_computation.252 | loop fusion | flops 58711296 | bytes 29417472 | tf_op jit(solution)/shard_map/reduce_sum | solution.py:260
  546.9 9.2 %broadcast_multiply_fusion.3 = (f32[2,512,1792]{1,2,0:T(8,128)S(1)}, f32[2,512,1792]{1,2,0:T(8,128)}, f32[2,512,1792]{1,2,0:T(8,128)}, f32[2,512,1792]{1,2,0:T(8,128)}) fusion(f32[2,512,1792]{1,2,0:T(8,128)S(1)} %get-tuple-element.278, f32[1792]{0:T(1024)S(1)} %copy-done.40, f32[1792]{0:T(1024)} %copy-done.41, f32[1792]{0:T(1024)} %copy-done.42, ...), kind=kLoop, calls=%fused_computation.155 | loop fusion | flops 7340032 | bytes 36728832 | tf_op jit(solution)/shard_map/mul | solution.py:274
  556.0 11.4 %pad_add_fusion = f32[2,515,1792]{1,2,0:T(8,128)S(1)} fusion(f32[2,512,1792]{1,2,0:T(8,128)} %get-tuple-element.296, f32[2,512,1792]{1,2,0:T(8,128)} %get-tuple-element.297, f32[2,512,1792]{1,2,0:T(8,128)} %get-tuple-element.298, f32[2,512,1792]{1,2,0:T(8,128)S(1)} %get-tuple-element.295), kind=kLoop, calls=%fused_computation.81 | loop fusion | flops 5537280 | bytes 36743168 | tf_op jit(solution)/shard_map/add | solution.py:271
  576.3 17.5 %collective-permute-done.7 = bf16[2,3,1792]{2,0,1:T(2,128)(2,1)S(1)} collective-permute-done((bf16[2,3,1792]{2,0,1:T(2,128)(2,1)S(1)}, bf16[2,3,1792]{2,0,1:T(2,128)(2,1)S(1)}, u32[]{:S(2)}, u32[]{:S(2)}) %collective-permute-start.7) | collective-permute-done | bytes 21536 | tf_op jit(solution)/shard_map/ppermute | solution.py:19
  602.6 12.1 %convolution_bitcast_fusion.2 = f32[768,3352]{1,0:T(8,128)} fusion(bf16[2,512,24]{1,2,0:T(8,128)(2,1)S(1)} %get-tuple-element.277, bf16[2,512,1792]{1,2,0:T(8,128)(2,1)S(1)} %fusion.71, bf16[2,512,1536]{1,2,0:T(8,128)(2,1)} %get-tuple-element.293, bf16[2,512,768]{2,1,0:T(8,128)(2,1)S(1)} %copy-done.12, f32[768]{0:T(1024)S(1)} %copy-done.62, ...), kind=kOutput, calls=%fused_computation.94 | convolution fusion | flops 5295980544 | bytes 18742272 | tf_op jit(solution)/shard_map/td,te->de/dot_general | solution.py:290
  627.0 11.0 %fusion.99 = (f32[768]{0:T(1024)S(1)}, f32[2,512]{1,0:T(2,128)S(1)}, f32[2,512,768]{2,1,0:T(8,128)}) fusion(bf16[2,512,768]{2,1,0:T(8,128)(2,1)S(1)} %copy-done.13, f32[2,512]{1,0:T(2,128)S(1)} %copy-done.60, f32[768]{0:T(1024)S(1)} %copy-done.62, bf16[768,3352]{1,0:T(8,128)(2,1)} %all-gather.4.cloned.1.call-done, ...), kind=kOutput, calls=%fused_computation.166 | convolution fusion | flops 5298337792 | bytes 16746496 | tf_op jit(solution)/shard_map/te,de->td/dot_general | solution.py:291
  638.1 38.9 %all-reduce.13 = (f32[768]{0:T(1024)S(1)}, f32[4,1792]{1,0:T(4,128)S(1)}, f32[1792]{0:T(1024)S(1)}, f32[24]{0:T(128)}, f32[24]{0:T(128)}, /*index=5*/f32[24]{0:T(128)}, f32[1536]{0:T(1024)S(1)}) all-reduce(f32[768]{0:T(1024)S(1)} %get-tuple-element.222, ...), channel_id=2, replica_groups=mesh['dp'=8,'seq'=4] {'dp','seq'}, use_global_device_ids=true, to_apply=%region_19.20.clone | all-reduce | flops 11336 | bytes 90688
  682.7 72.5 %reduce-scatter.8.cloned.1.call-done = f32[24,3352]{1,0:T(8,128)} async-done(((f32[768,3352]{1,0:T(8,128)}), f32[24,3352]{1,0:T(8,128)}) %reduce-scatter.8.cloned.1.call-update) | async-done | bytes 321808
  (368 shorter events, 325.6 us)
Async XLA Ops:
  7.2 91.2 %all-gather.4.cloned.1.call-start = ((), (), s32[]{:S(2)}) async-start(), calls=%async_computation.2 | async-start | bytes 5474304 | tf_op jit(solution)/shard_map/all_gather | solution.py:88
  8.9 273.9 %all-gather.6.cloned.1.call-start = ((), (), s32[]{:S(2)}) async-start(), calls=%async_computation.3 | async-start | bytes 2433024 | tf_op jit(solution)/shard_map/all_gather | solution.py:92
  9.6 103.8 %copy-start.72 = (f32[24]{0:T(128)}, f32[24]{0:T(128)S(1)}, u32[]{:S(2)}) copy-start(f32[24]{0:T(128)S(1)} %exp.45) | copy-start | bytes 292
  54.5 56.7 %copy-start.61 = (f32[768]{0:T(1024)}, f32[768]{0:T(1024)S(1)}, u32[]{:S(2)}) copy-start(f32[768]{0:T(1024)S(1)} %convert_element_type.157) | copy-start | bytes 9220
  96.0 31.3 %copy-start.39 = (f32[1792]{0:T(1024)}, f32[1792]{0:T(1024)S(1)}, u32[]{:S(2)}) copy-start(f32[1792]{0:T(1024)S(1)} %get-tuple-element.224) | copy-start | bytes 21508
  116.3 79.6 %copy-start.44 = (f32[4,24,2]{1,2,0:T(2,128)}, f32[4,24,2]{1,2,0:T(2,128)S(1)}, u32[]{:S(2)}) copy-start(f32[4,24,2]{1,2,0:T(2,128)S(1)} %copy.167) | copy-start | bytes 2308
  116.7 52.7 %copy-start.63 = (f32[2,1,24]{2,1,0:T(1,128)}, f32[2,1,24]{2,1,0:T(1,128)S(1)}, u32[]{:S(2)}) copy-start(f32[2,1,24]{2,1,0:T(1,128)S(1)} %get-tuple-element.311) | copy-start | bytes 580
  119.1 7.7 %collective-permute-start = (bf16[2,3,1792]{2,0,1:T(2,128)(2,1)S(1)}, bf16[2,3,1792]{2,0,1:T(2,128)(2,1)S(1)}, u32[]{:S(2)}, u32[]{:S(2)}) collective-permute-start(bf16[2,3,1792]{2,0,1:T(2,128)(2,1)S(1)} %copy.158), channel_id=1, source_target_pairs={{0,1},{1,2},{2,3},{4,5},{5,6},{6,7},{8,9},{9,10},{10,11},{12,13},{... | collective-permute-start | bytes 64520 | tf_op jit(solution)/shard_map/ppermute | solution.py:19
  121.9 218.2 %copy-start.54 = (f32[2,24]{1,0:T(2,128)}, f32[2,24]{1,0:T(2,128)S(1)}, u32[]{:S(2)}) copy-start(f32[2,24]{1,0:T(2,128)S(1)} %get-tuple-element.286) | copy-start | bytes 580
  169.8 4.9 collective-permute-start.1
  176.1 24.5 %collective-permute-start.2 = (f32[2,24,128,64]{2,3,1,0:T(8,128)}, f32[2,24,128,64]{2,3,1,0:T(8,128)}, u32[]{:S(2)}, u32[]{:S(2)}) collective-permute-start(f32[2,24,128,64]{2,3,1,0:T(8,128)} %multiply_add_fusion.3), channel_id=1, source_target_pairs={{0,1},{1,2},{2,3},{4,5},{5,6},{6,7},{8,9},{9,10},{10,11},{12,13},{... | collective-permute-start | bytes 4718600 | tf_op jit(solution)/shard_map/ppermute | solution.py:19
  194.1 488.6 %reduce-scatter.6.cloned.1.call-start = ((), (), s32[]{:S(2)}) async-start(), calls=%async_computation.4 | async-start | bytes 4866048 | tf_op jit(solution)/shard_map/reduce_scatter | solution.py:306
  194.2 99.3 %copy-start.52 = (f32[1536]{0:T(1024)}, f32[1536]{0:T(1024)S(1)}, u32[]{:S(2)}) copy-start(f32[1536]{0:T(1024)S(1)} %convert_element_type.172) | copy-start | bytes 18436
  194.3 88.5 %copy-start.68 = (f32[2,512]{1,0:T(2,128)}, f32[2,512]{1,0:T(2,128)S(1)}, u32[]{:S(2)}) copy-start(f32[2,512]{1,0:T(2,128)S(1)} %compare_convert_fusion) | copy-start | bytes 12292
  203.8 45.1 %collective-permute-start.3 = (f32[2,24,128,64]{2,3,1,0:T(8,128)}, f32[2,24,128,64]{2,3,1,0:T(8,128)}, u32[]{:S(2)}, u32[]{:S(2)}) collective-permute-start(f32[2,24,128,64]{2,3,1,0:T(8,128)} %multiply_add_fusion.2), channel_id=1, source_target_pairs={{0,1},{1,2},{2,3},{4,5},{5,6},{6,7},{8,9},{9,10},{10,11},{12,13},{... | collective-permute-start | bytes 4718600 | tf_op jit(solution)/shard_map/ppermute | solution.py:19
  333.9 6.2 collective-permute-start.4
  341.4 22.1 %collective-permute-start.5 = (f32[2,24,128,64]{2,3,1,0:T(8,128)}, f32[2,24,128,64]{2,3,1,0:T(8,128)}, u32[]{:S(2)}, u32[]{:S(2)}) collective-permute-start(f32[2,24,128,64]{2,3,1,0:T(8,128)} %multiply_add_fusion.1), channel_id=1, source_target_pairs={{1,0},{2,1},{3,2},{5,4},{6,5},{7,6},{9,8},{10,9},{11,10},{13,12},{... | collective-permute-start | bytes 4718600 | tf_op jit(solution)/shard_map/ppermute | solution.py:19
  356.8 398.4 %reduce-scatter.8.cloned.1.call-start = ((), (), s32[]{:S(2)}) async-start(), calls=%async_computation.5 | async-start | bytes 10948608
  366.8 88.7 %collective-permute-start.6 = (f32[2,24,128,64]{2,3,1,0:T(8,128)}, f32[2,24,128,64]{2,3,1,0:T(8,128)}, u32[]{:S(2)}, u32[]{:S(2)}) collective-permute-start(f32[2,24,128,64]{2,3,1,0:T(8,128)} %multiply_add_fusion), channel_id=1, source_target_pairs={{1,0},{2,1},{3,2},{5,4},{6,5},{7,6},{9,8},{10,9},{11,10},{13,12},{... | collective-permute-start | bytes 4718600 | tf_op jit(solution)/shard_map/ppermute | solution.py:19
  371.4 65.3 %copy-start.36 = (f32[4,24,256]{2,1,0:T(8,128)S(1)}, f32[4,24,256]{2,1,0:T(8,128)}, u32[]{:S(2)}) copy-start(f32[4,24,256]{2,1,0:T(8,128)} %fusion.129) | copy-start | bytes 294916
  573.6 20.2 %collective-permute-start.7 = (bf16[2,3,1792]{2,0,1:T(2,128)(2,1)S(1)}, bf16[2,3,1792]{2,0,1:T(2,128)(2,1)S(1)}, u32[]{:S(2)}, u32[]{:S(2)}) collective-permute-start(bf16[2,3,1792]{2,0,1:T(2,128)(2,1)S(1)} %copy.199), channel_id=1, source_target_pairs={{1,0},{2,1},{3,2},{5,4},{6,5},{7,6},{9,8},{10,9},{11,10},{13,12},{... | collective-permute-start | bytes 64520 | tf_op jit(solution)/shard_map/ppermute | solution.py:19
  627.0 52.3 %copy-start.14 = (bf16[2,512,768]{2,1,0:T(8,128)(2,1)S(1)}, bf16[2,512,768]{2,1,0:T(8,128)(2,1)}, u32[]{:S(2)}) copy-start(bf16[2,512,768]{2,1,0:T(8,128)(2,1)} %param.18) | copy-start | bytes 4718596
  627.0 52.3 %copy-start.29 = (bf16[2,512,768]{2,1,0:T(8,128)(2,1)S(1)}, bf16[2,512,768]{2,1,0:T(8,128)(2,1)}, u32[]{:S(2)}) copy-start(bf16[2,512,768]{2,1,0:T(8,128)(2,1)} %param.29) | copy-start | bytes 4718596
  627.0 52.3 %copy-start.58 = (f32[2,512]{1,0:T(2,128)S(1)}, f32[2,512]{1,0:T(2,128)}, u32[]{:S(2)}) copy-start(f32[2,512]{1,0:T(2,128)} %get-tuple-element.307) | copy-start | bytes 12292
  (67 other events, 677.3 us)
Sparse Core Ops, SparseCore 0:
  11.5 68.4 all-gather.3
  194.2 55.1 all-gather.5
  356.9 123.3 reduce-scatter.5
  614.9 140.2 reduce-scatter.7
where the time goes:
time: 772 us; the launch traced here: 762 us
  matrix products  187 us (24%)
  local copies, waits for them, and re-layouts  151 us (20%)
  other arithmetic  139 us (18%)
  blocking collectives  122 us (16%)
  waiting for transfers between devices  105 us (14%)
  starting transfers between devices  43.2 us (6%)
  between operations  15.5 us (2%)
    unnamed x2, blocking collectives  81.2 us
    unnamed x5, waiting for transfers between devices  72.5 us
    ppermute x8, starting transfers between devices, from_behind(): return lax.ppermute(block, axis, route)  43 us
    all_gather x1, blocking collectives, per_device(): lax.all_gather(shards[2], ('dp', 'seq'), axis=1, tiled=True)  40.5 us
    another operation x12, other arithmetic  39.2 us
    ppermute x8, waiting for transfers between devices, from_behind(): return lax.ppermute(block, axis, route)  32 us
    dot_general x4, matrix products, intra_backward(): jnp.einsum('qhp,rhp->hqr', grad_group, x_group, preferred_element_type=jn...  22 us
    reduce_sum x1, other arithmetic, per_device(): grad_conv_bias = jnp.sum(grad_pre, axis=(0, 1))  19.6 us
  transfers between devices with their start and end apart: 12, of which 5 were waited for; matrix products, arithmetic and copies ran while one was open for 46% of the time, Pallas kernels for 0%

commit v1 on v0

--- a/solution.py
+++ b/solution.py
@@ -11,6 +11,28 @@
 DI = 1536
 CD = 1792
 epsilon = 1e-05
+
+
+def laid_out(blocks, dim):
+    blocks = jnp.moveaxis(blocks, 0, dim)
+    dims = blocks.shape
+    return blocks.reshape(*dims[:dim], dims[dim] * dims[dim + 1], *dims[dim + 2 :])
+
+
+def collected_by_bits(x, axis):
+    size = lax.axis_size(axis)
+    parts = x[None]
+    for level in range(size.bit_length() - 1):
+        distance = 1 << level
+        theirs = lax.ppermute(parts, axis, [(i, i ^ distance) for i in range(size)])
+        both = jnp.stack([parts, theirs])
+        upper = lax.axis_index(axis) >> level & 1
+        parts = jnp.where(upper == 0, both, both[::-1]).reshape(-1, *x.shape)
+    return parts
+
+
+def doubled_up(x, axis, dim):
+    return laid_out(collected_by_bits(x, axis), dim)
 
 
 def from_behind(block, axis, distance):
@@ -86,7 +108,7 @@
     gathered = (
         lax.all_gather(shards[0], ("dp", "seq"), axis=0, tiled=True),
         lax.all_gather(shards[1], ("dp", "seq"), axis=0, tiled=True),
-        lax.all_gather(shards[2], ("dp", "seq"), axis=1, tiled=True),
+        doubled_up(shards[2], ("dp", "seq"), 1),
         lax.all_gather(shards[3], ("dp", "seq"), axis=0, tiled=True),
         lax.all_gather(shards[4], ("dp", "seq"), axis=0, tiled=True),
         lax.all_gather(shards[5], ("dp", "seq"), axis=0, tiled=True),

time: 772 us -> 811 us (1.051)
  blocking collectives: 122 us -> 147 us
  starting transfers between devices: 43.2 us -> 55.1 us
  waiting for transfers between devices: 105 us -> 94 us
    all_gather x1, blocking collectives: 40.5 us -> 65.7 us  [per_device(): lax.all_gather(back_shards[2], ('dp', 'seq'), axis=1, tiled=True)]
    ppermute x8, waiting for transfers between devices: 32 us -> 8.63 us  [from_behind(): return lax.ppermute(block, axis, route)]
    ppermute x0 -> x5, starting transfers between devices: none -> 10.5 us  [collected_by_bits(): theirs = lax.ppermute(parts, axis, [(i, i ^ distance) for i in range(size)])]
    all_gather x1, waiting for transfers between devices: 0.01 us -> 8.77 us  [per_device(): lax.all_gather(shards[1], ('dp', 'seq'), axis=0, tiled=True)]
    another operation x12 -> x18, other arithmetic: 39.2 us -> 39.3 us
  transfers between devices with their start and end apart: 12 -> 17, of which waited for: 5 -> 8; matrix products, arithmetic and copies ran while one was open for 46% -> 45% of each run, Pallas kernels for 0% -> 0%
where the time goes in v1:
time: 811 us; the launch traced here: 800 us
  matrix products  190 us (23%)
  local copies, waits for them, and re-layouts  158 us (19%)
  blocking collectives  147 us (18%)
  other arithmetic  141 us (17%)
  waiting for transfers between devices  94 us (12%)
  starting transfers between devices  55.1 us (7%)
  between operations  15.5 us (2%)
    unnamed x2, blocking collectives  81.1 us
    unnamed x5, waiting for transfers between devices  72.6 us
    all_gather x1, blocking collectives, per_device(): lax.all_gather(back_shards[2], ('dp', 'seq'), axis=1, tiled=True)  65.7 us
    ppermute x8, starting transfers between devices, from_behind(): return lax.ppermute(block, axis, route)  44.5 us
    another operation x12, other arithmetic  39.2 us
    dot_general x4, matrix products, intra_backward(): jnp.einsum('qhp,rhp->hqr', grad_group, x_group, preferred_element_type=jn...  22 us
    reduce_sum x1, other arithmetic, per_device(): grad_conv_bias = jnp.sum(grad_pre, axis=(0, 1))  19.2 us
    dot_general x4, matrix products, intra_forward(): jnp.einsum('hqr,rhp->qhp', mixing, x_group, preferred_element_type=jnp.fl...  17.6 us
  transfers between devices with their start and end apart: 17, of which 8 were waited for; matrix products, arithmetic and copies ran while one was open for 45% of the time, Pallas kernels for 0%

profile of v1, /device:TPU:0, one launch (start us, length us, event | category | flops | bytes accessed | tf_op | source)
XLA Modules:
  0.0 799.7 jit_solution(4673710329352124289)
XLA Ops:
  29.9 41.2 %all-reduce.14 = (bf16[768]{0:T(1024)(128)(2,1)S(1)}, bf16[1792]{0:T(1024)(128)(2,1)S(1)}, bf16[1536]{0:T(1024)(128)(2,1)S(1)}) all-reduce(bf16[768]{0:T(1024)(128)(2,1)S(1)} %dynamic-update-slice.4, bf16[1792]{0:T(1024)(128)(2,1)S(1)} %dynamic-update-slice.3, ...), channel_id=1, replica_groups=mesh['dp'=8,'seq'=4] {'dp','seq'}, use_global_device_ids=true, to_apply=%add.6 | all-reduce | flops 4096 | bytes 16384
  71.8 8.8 %all-gather.4.cloned.1.call-done = bf16[768,3352]{1,0:T(8,128)(2,1)} async-done(((bf16[24,3352]{1,0:T(8,128)(2,1)}), bf16[768,3352]{1,0:T(8,128)(2,1)}) %all-gather.4.cloned.1.call-update) | async-done | bytes 5148688 | tf_op jit(solution)/shard_map/all_gather | solution.py:110
  80.6 15.2 %fusion.147 = (bf16[2,512,3352]{1,2,0:T(8,128)(2,1)}, f32[2,512,3352]{1,2,0:T(8,128)S(1)}) fusion(bf16[768,3352]{1,0:T(8,128)(2,1)} %all-gather.4.cloned.1.call-done, bf16[2,512,768]{2,1,0:T(8,128)(2,1)} %param.18, f32[768]{0:T(1024)S(1)} %convert_element_type.168, f32[2,512]{1,0:T(2,128)S(1)} %get-tuple-element.312), kind=kOutput, calls=%fused_computation.275 | convolution fusion | flops 5278818304 | bytes 27323392 | tf_op jit(solution)/shard_map/dot_general | solution.py:126
  115.8 12.4 %multiply_convert_fusion.14 = (bf16[2,512,1792]{1,2,0:T(8,128)(2,1)S(1)}, f32[2,512,1792]{1,2,0:T(8,128)}) fusion(bf16[2,512,1792]{1,2,0:T(8,128)(2,1)} %slice.170, f32[1792]{0:T(1024)S(1)} %mul.546, bf16[2,3,1792]{1,2,0:T(8,128)(2,1)S(1)} %copy.158, f32[1792]{0:T(1024)S(1)} %mul.543, f32[1792]{0:T(1024)S(1)} %mul.540, f32[1792]{0:T(1024)S(1)} %mul.532, ...), kind=kLoop, calls=%fused_computation.107 | loop fusion | flops 47710208 | bytes 14737408 | tf_op jit(solution)/shard_map/convert.10
  129.3 14.5 %copy.159 = bf16[2,512,1536]{1,0,2:T(2,128)(2,1)} copy(bf16[2,512,1536]{1,2,0:T(8,128)(2,1)S(1)} %slice.178) | data formatting | bytes 6291456 | tf_op jit(solution)/shard_map/slice | solution.py:142
  165.8 17.7 %collective-permute-start.7 = (f32[2,24,128,64]{2,3,1,0:T(8,128)}, f32[2,24,128,64]{2,3,1,0:T(8,128)}, u32[]{:S(2)}, u32[]{:S(2)}) collective-permute-start(f32[2,24,128,64]{2,3,1,0:T(8,128)} %multiply_add_fusion.3), channel_id=1, source_target_pairs={{0,1},{1,2},{2,3},{4,5},{5,6},{6,7},{8,9},{9,10},{10,11},{12,13},{... | collective-permute-start | bytes 4718600 | tf_op jit(solution)/shard_map/ppermute | solution.py:41
  194.0 15.5 %collective-permute-start.8 = (f32[2,24,128,64]{2,3,1,0:T(8,128)}, f32[2,24,128,64]{2,3,1,0:T(8,128)}, u32[]{:S(2)}, u32[]{:S(2)}) collective-permute-start(f32[2,24,128,64]{2,3,1,0:T(8,128)} %multiply_add_fusion.2), channel_id=1, source_target_pairs={{0,1},{1,2},{2,3},{4,5},{5,6},{6,7},{8,9},{9,10},{10,11},{12,13},{... | collective-permute-start | bytes 4718600 | tf_op jit(solution)/shard_map/ppermute | solution.py:41
  212.9 24.9 %while.29 = (s32[]{:T(128)}, f32[4,256,24,64]{1,3,2,0:T(8,128)}, bf16[4,256,24,64]{1,3,2,0:T(8,128)(2,1)}, bf16[4,256,128]{2,1,0:T(8,128)(2,1)}, bf16[4,256,128]...) while((s32[]{:T(128)}, f32[4,256,24,64]{1,3,2,0:T(8,128)}, ...), condition=%wide.region_4.5_spmd, body=%wide.region_3.4_spmd.sunk | while | flops 227606528 | bytes 3319905 | solution.py:149
  255.8 9.3 %reshape.347 = f32[2,512,1536]{1,0,2:T(2,128)} reshape(f32[4,256,24,64]{1,0,3,2:T(4,128)} %copy.178) | data formatting | bytes 12582912 | tf_op jit(solution)/shard_map/reshape | solution.py:184
  272.8 10.6 %multiply_reduce_fusion.3 = (f32[1536]{0:T(1024)}, f32[2,512]{1,0:T(2,128)S(1)}, f32[2,512,1536]{1,2,0:T(8,128)}) fusion(f32[2,512,1536]{1,2,0:T(8,128)} %get-tuple-element.286, f32[2,512]{1,0:T(2,128)S(1)} %get-tuple-element.314, f32[1536]{0:T(1024)S(1)} %convert_element_type.183, bf16[1536,768]{1,0:T(8,128)(2,1)} %all-gather.6.cloned.1.call-done, ...), kind=kOutput, calls=%fused_computation.121 | convolution fusion | flops 2427713024 | bytes 16539648 | tf_op jit(solution)/shard_map/td,kd->tk/dot_general | solution.py:212
  283.4 8.8 %multiply_convert_fusion.16 = (bf16[2,512,1536]{1,2,0:T(8,128)(2,1)}, bf16[2,512,1536]{1,2,0:T(8,128)(2,1)S(1)}) fusion(f32[2,512,1536]{1,0,2:T(2,128)S(1)} %copy-done, f32[2,512,3352]{1,2,0:T(8,128)} %copy-done.7, f32[2,512]{1,0:T(2,128)S(1)} %broadcast_multiply_fusion.4, f32[2,512,1536]{1,2,0:T(8,128)S(1)} %copy-done.2, ...), kind=kLoop, calls=%fused_computation.123 | loop fusion | flops 28311552 | bytes 31475712 | tf_op jit(solution)/shard_map/convert.4
  292.1 14.4 %copy.184 = bf16[2,512,1536]{1,0,2:T(2,128)(2,1)} copy(bf16[2,512,1536]{1,2,0:T(8,128)(2,1)S(1)} %get-tuple-element.298) | data formatting | bytes 6291456 | tf_op jit(solution)/shard_map/convert_element_type | solution.py:220
  332.5 65.7 %all-gather = bf16[32,56,4]{1,2,0:T(4,128)(2,1)S(1)} all-gather(bf16[1,56,4]{1,2,0:T(4,128)(2,1)S(1)} %get-tuple-element.315), channel_id=1, replica_groups=mesh['dp'=8,'seq'=4] {'dp','seq'}, dimensions={0}, use_global_device_ids=true | all-gather | bytes 14784 | tf_op jit(solution)/shard_map/all_gather | solution.py:201
  422.6 61.4 %while.30 = (s32[]{:T(128)}, f32[4,256,24,64]{1,3,2,0:T(8,128)}, f32[4,256,128]{2,1,0:T(8,128)}, f32[4,256,128]{2,1,0:T(8,128)}, f32[4,24,256]{2,1,0:T(8,128)}, ...) while((s32[]{:T(128)}, f32[4,256,24,64]{1,3,2,0:T(8,128)}, ...), condition=%wide.region_12.13_spmd, body=%wide.region_7.12_spmd.sunk | while | flops 481284096 | bytes 6280337 | solution.py:224
  487.8 11.1 %fusion.52 = (f32[4,24,256]{2,1,0:T(8,128)}, bf16[4,24,256,128]{3,2,1,0:T(8,128)(2,1)S(1)}) fusion(f32[4,24,256]{2,1,0:T(8,128)S(1)} %copy-done.37, f32[4,256,128]{2,1,0:T(8,128)} %copy-done.24, bf16[4,24,128,64]{2,3,1,0:T(8,128)(2,1)} %bitcast.312, bf16[4,256,24,64]{1,0,3,2:T(4,128)(2,1)} %reshape.348), kind=kOutput, calls=%fused_computation.73 | convolution fusion | flops 415211520 | bytes 11730944 | tf_op jit(solution)/shard_map/bqhp,bhnp->bhqn/dot_general | solution.py:260
  542.2 9.4 %reshape.350 = f32[2,512,1536]{1,0,2:T(2,128)} reshape(f32[4,256,24,64]{1,0,3,2:T(4,128)} %copy.193) | data formatting | bytes 12582912 | tf_op jit(solution)/shard_map/reshape | solution.py:274
  562.3 10.0 %reduce-window.16 = f32[4,24,2,128]{3,1,2,0:T(8,128)S(1)} reduce-window(f32[4,24,2,128]{3,1,2,0:T(8,128)S(1)} %copy.206, f32[]{:T(128)} %constant.105.clone.1), window={size=1x1x1x128 pad=0_0x0_0x0_0x0_127}, to_apply=%region_15.16 | reduce-window | flops 3121152 | bytes 196612 | tf_op jit(solution)/shard_map/reduce-window.2
  578.0 19.2 %fusion.139 = (f32[1792]{0:T(1024)S(1)}, f32[1792]{0:T(1024)S(1)}, f32[1792]{0:T(1024)S(1)}, f32[1792]{0:T(1024)S(1)}, f32[1792]{0:T(1024)S(1)}, /*index=5*/f32[2,512,1792]{1,2,0:T(8,128)S(1)}) fusion(bf16[2,512,3352]{1,2,0:T(8,128)(2,1)} %get-tuple-element.324, bf16[2,512,1792]{1,2,0:T(8,128)(2,1)} %slice.170, bf16[2,3,1792]{1,2,0:T(8,128)(2,1)} %copy-done.9, ...), kind=kLoop, calls=%fused_computation.271 | loop fusion | flops 58711296 | bytes 29417472 | tf_op jit(solution)/shard_map/reduce_sum | solution.py:282
  597.2 10.6 %broadcast_multiply_fusion.3 = (f32[2,512,1792]{1,2,0:T(8,128)}, f32[2,512,1792]{1,2,0:T(8,128)}, f32[2,512,1792]{1,2,0:T(8,128)}, f32[2,512,1792]{1,2,0:T(8,128)}) fusion(f32[2,512,1792]{1,2,0:T(8,128)S(1)} %get-tuple-element.282, f32[1792]{0:T(1024)S(1)} %copy-done.43, f32[1792]{0:T(1024)S(1)} %copy-done.44, f32[1792]{0:T(1024)S(1)} %copy-done.45, ...), kind=kLoop, calls=%fused_computation.155 | loop fusion | flops 7340032 | bytes 36728832 | tf_op jit(solution)/shard_map/mul | solution.py:296
  607.9 12.7 %pad_add_fusion = f32[2,515,1792]{1,2,0:T(8,128)S(1)} fusion(f32[2,512,1792]{1,2,0:T(8,128)} %get-tuple-element.300, f32[2,512,1792]{1,2,0:T(8,128)} %get-tuple-element.301, f32[2,512,1792]{1,2,0:T(8,128)} %get-tuple-element.302, f32[2,512,1792]{1,2,0:T(8,128)} %get-tuple-element.299), kind=kLoop, calls=%fused_computation.81 | loop fusion | flops 5537280 | bytes 36743168 | tf_op jit(solution)/shard_map/add | solution.py:293
  639.1 12.2 %convolution_bitcast_fusion.2 = f32[768,3352]{1,0:T(8,128)} fusion(bf16[2,512,24]{1,2,0:T(8,128)(2,1)S(1)} %get-tuple-element.281, bf16[2,512,1792]{1,2,0:T(8,128)(2,1)S(1)} %fusion.71, bf16[2,512,1536]{1,2,0:T(8,128)(2,1)} %get-tuple-element.297, bf16[2,512,768]{2,1,0:T(8,128)(2,1)S(1)} %copy-done.13, f32[768]{0:T(1024)S(1)} %copy-done.57, ...), kind=kOutput, calls=%fused_computation.94 | convolution fusion | flops 5295980544 | bytes 18742272 | tf_op jit(solution)/shard_map/td,te->de/dot_general | solution.py:312
  663.5 11.1 %fusion.99 = (f32[768]{0:T(1024)S(1)}, f32[2,512]{1,0:T(2,128)S(1)}, f32[2,512,768]{2,1,0:T(8,128)}) fusion(bf16[2,512,768]{2,1,0:T(8,128)(2,1)S(1)} %copy-done.14, f32[2,512]{1,0:T(2,128)S(1)} %copy-done.55, f32[768]{0:T(1024)S(1)} %copy-done.57, bf16[768,3352]{1,0:T(8,128)(2,1)} %all-gather.4.cloned.1.call-done, ...), kind=kOutput, calls=%fused_computation.166 | convolution fusion | flops 5298337792 | bytes 16746496 | tf_op jit(solution)/shard_map/te,de->td/dot_general | solution.py:313
  674.6 39.9 %all-reduce.13 = (f32[768]{0:T(1024)S(1)}, f32[4,1792]{1,0:T(4,128)S(1)}, f32[1792]{0:T(1024)S(1)}, f32[24]{0:T(128)}, f32[24]{0:T(128)}, /*index=5*/f32[24]{0:T(128)}, f32[1536]{0:T(1024)S(1)}) all-reduce(f32[768]{0:T(1024)S(1)} %get-tuple-element.222, ...), channel_id=2, replica_groups=mesh['dp'=8,'seq'=4] {'dp','seq'}, use_global_device_ids=true, to_apply=%region_19.20.clone | all-reduce | flops 11336 | bytes 90688
  720.2 72.5 %reduce-scatter.8.cloned.1.call-done = f32[24,3352]{1,0:T(8,128)} async-done(((f32[768,3352]{1,0:T(8,128)}), f32[24,3352]{1,0:T(8,128)}) %reduce-scatter.8.cloned.1.call-update) | async-done | bytes 321808
  (384 shorter events, 341.3 us)
Async XLA Ops:
  7.2 73.4 %all-gather.4.cloned.1.call-start = ((), (), s32[]{:S(2)}) async-start(), calls=%async_computation.2 | async-start | bytes 5474304 | tf_op jit(solution)/shard_map/all_gather | solution.py:110
  8.9 263.8 %all-gather.6.cloned.1.call-start = ((), (), s32[]{:S(2)}) async-start(), calls=%async_computation.3 | async-start | bytes 2433024 | tf_op jit(solution)/shard_map/all_gather | solution.py:114
  9.6 1.3 collective-permute-start
  10.9 4.4 collective-permute-start.1
  15.4 3.7 collective-permute-start.2
  19.1 4.0 collective-permute-start.3
  23.2 48.0 %collective-permute-start.4 = (bf16[16,4,56]{2,1,0:T(4,128)(2,1)S(1)}, bf16[16,4,56]{2,1,0:T(4,128)(2,1)S(1)}, u32[]{:S(2)}, u32[]{:S(2)}) collective-permute-start(bf16[16,4,56]{2,1,0:T(4,128)(2,1)S(1)} %bitcast.323), channel_id=1, source_target_pairs={{0,16},{1,17},{2,18},{3,19},{4,20},{5,21},{6,22},{7,23},{8,24},{9,... | collective-permute-start | bytes 21512 | tf_op jit(solution)/shard_map/ppermute | solution.py:27
  26.6 69.1 %copy-start.54 = (f32[2,512]{1,0:T(2,128)}, f32[2,512]{1,0:T(2,128)S(1)}, u32[]{:S(2)}) copy-start(f32[2,512]{1,0:T(2,128)S(1)} %get-tuple-element.312) | copy-start | bytes 12292
  27.3 74.6 %copy-start.67 = (f32[24]{0:T(128)}, f32[24]{0:T(128)S(1)}, u32[]{:S(2)}) copy-start(f32[24]{0:T(128)S(1)} %exp.45) | copy-start | bytes 292
  104.8 81.1 %copy-start.40 = (f32[4,24,2]{1,2,0:T(2,128)}, f32[4,24,2]{1,2,0:T(2,128)S(1)}, u32[]{:S(2)}) copy-start(f32[4,24,2]{1,2,0:T(2,128)S(1)} %copy.166) | copy-start | bytes 2308
  107.8 7.6 collective-permute-start.5
  110.5 219.3 %copy-start.49 = (f32[2,24]{1,0:T(2,128)}, f32[2,24]{1,0:T(2,128)S(1)}, u32[]{:S(2)}) copy-start(f32[2,24]{1,0:T(2,128)S(1)} %get-tuple-element.290) | copy-start | bytes 580
  158.2 6.2 collective-permute-start.6
  165.8 24.9 %collective-permute-start.7 = (f32[2,24,128,64]{2,3,1,0:T(8,128)}, f32[2,24,128,64]{2,3,1,0:T(8,128)}, u32[]{:S(2)}, u32[]{:S(2)}) collective-permute-start(f32[2,24,128,64]{2,3,1,0:T(8,128)} %multiply_add_fusion.3), channel_id=1, source_target_pairs={{0,1},{1,2},{2,3},{4,5},{5,6},{6,7},{8,9},{9,10},{10,11},{12,13},{... | collective-permute-start | bytes 4718600 | tf_op jit(solution)/shard_map/ppermute | solution.py:41
  184.2 536.0 %reduce-scatter.6.cloned.1.call-start = ((), (), s32[]{:S(2)}) async-start(), calls=%async_computation.4 | async-start | bytes 4866048 | tf_op jit(solution)/shard_map/reduce_scatter | solution.py:328
  184.2 99.1 %copy-start.47 = (f32[1536]{0:T(1024)}, f32[1536]{0:T(1024)S(1)}, u32[]{:S(2)}) copy-start(f32[1536]{0:T(1024)S(1)} %convert_element_type.183) | copy-start | bytes 18436
  184.3 88.4 %copy-start.63 = (f32[2,512]{1,0:T(2,128)}, f32[2,512]{1,0:T(2,128)S(1)}, u32[]{:S(2)}) copy-start(f32[2,512]{1,0:T(2,128)S(1)} %compare_convert_fusion) | copy-start | bytes 12292
  194.0 44.9 %collective-permute-start.8 = (f32[2,24,128,64]{2,3,1,0:T(8,128)}, f32[2,24,128,64]{2,3,1,0:T(8,128)}, u32[]{:S(2)}, u32[]{:S(2)}) collective-permute-start(f32[2,24,128,64]{2,3,1,0:T(8,128)} %multiply_add_fusion.2), channel_id=1, source_target_pairs={{0,1},{1,2},{2,3},{4,5},{5,6},{6,7},{8,9},{9,10},{10,11},{12,13},{... | collective-permute-start | bytes 4718600 | tf_op jit(solution)/shard_map/ppermute | solution.py:41
  323.8 6.0 collective-permute-start.9
  331.2 83.4 %collective-permute-start.10 = (f32[2,24,128,64]{2,3,1,0:T(8,128)}, f32[2,24,128,64]{2,3,1,0:T(8,128)}, u32[]{:S(2)}, u32[]{:S(2)}) collective-permute-start(f32[2,24,128,64]{2,3,1,0:T(8,128)} %multiply_add_fusion.1), channel_id=1, source_target_pairs={{1,0},{2,1},{3,2},{5,4},{6,5},{7,6},{9,8},{10,9},{11,10},{13,12},{... | collective-permute-start | bytes 4718600 | tf_op jit(solution)/shard_map/ppermute | solution.py:41
  414.5 378.2 %reduce-scatter.8.cloned.1.call-start = ((), (), s32[]{:S(2)}) async-start(), calls=%async_computation.5 | async-start | bytes 10948608
  417.9 88.8 %collective-permute-start.11 = (f32[2,24,128,64]{2,3,1,0:T(8,128)}, f32[2,24,128,64]{2,3,1,0:T(8,128)}, u32[]{:S(2)}, u32[]{:S(2)}) collective-permute-start(f32[2,24,128,64]{2,3,1,0:T(8,128)} %multiply_add_fusion), channel_id=1, source_target_pairs={{1,0},{2,1},{3,2},{5,4},{6,5},{7,6},{9,8},{10,9},{11,10},{13,12},{... | collective-permute-start | bytes 4718600 | tf_op jit(solution)/shard_map/ppermute | solution.py:41
  422.6 65.2 %copy-start.37 = (f32[4,24,256]{2,1,0:T(8,128)S(1)}, f32[4,24,256]{2,1,0:T(8,128)}, u32[]{:S(2)}) copy-start(f32[4,24,256]{2,1,0:T(8,128)} %fusion.131) | copy-start | bytes 294916
  626.6 3.6 collective-permute-start.12
  (67 other events, 792.4 us)
Sparse Core Ops, SparseCore 0:
  11.5 68.9 all-gather.3
  184.3 56.8 all-gather.5
  414.7 107.2 reduce-scatter.5
  651.5 141.1 reduce-scatter.7
